TPU v7x, 256 devices: a whole 4x4x8 slice. The times are simulated.
256 devices in a mesh: seq: 32 (over x, y, core), dp: 8 (over z).
Axes of the slice: x: 4, y: 4, z: 8, core: 2. Of those that a mesh axis runs over, the one named last changes fastest.
Arguments:
- queries: bfloat16 [8, 16384, 2048], P('dp', 'seq'), may hold values from -5 to 5
- keys: bfloat16 [8, 16384, 2048], P('dp', 'seq'), may hold values from -5 to 5
- values: bfloat16 [8, 16384, 2048], P('dp', 'seq'), may hold values from -8 to 8
- out_weight: bfloat16 [2048, 4096], P(None, 'dp'), may hold values from -0.125 to 0.125
Outputs:
- projected: bfloat16 [8, 16384, 4096], P('dp', 'seq')
All inputs are finite; a program needn't handle non-finite values.
Results may differ from a plain program's by a relative error of at most 0.0061.
Values may be sent and summed in bfloat16 or wider, within the bound.
No kernel may reach another device: no remote copies, remote signals or barrier semaphores. Data moves between devices by JAX's collectives and lax.ppermute only.
A program may use at most 192 MiB of HBM per device.

v0:
```python
import math
import jax
import jax.numpy as jnp
from jax import lax
from jax.sharding import PartitionSpec as P

CHANNEL_WIDTH = 128
SEGMENT_LENGTH = 256


def prefix(value, axis, join, neutral):
    count, mine = (lax.axis_size(axis), lax.axis_index(axis))
    pieces = jax.tree.map(lambda part: lax.all_gather(part, axis), value)
    subtotal = jax.tree.map(
        lambda part, zero: jnp.full_like(part, 0) + jnp.asarray(zero, part.dtype), value, neutral
    )

    def turn(position, subtotal):
        longer = join(subtotal, jax.tree.map(lambda part: part[position], pieces))
        return jax.tree.map(lambda new, old: jnp.where(position < mine, new, old), longer, subtotal)

    return lax.fori_loop(0, count - 1, turn, subtotal)


def shifted(block, axis, distance):
    devices = range(lax.axis_size(axis))
    route = [(i - distance, i) for i in devices if i - distance in devices]
    return lax.ppermute(block, axis, route)


def add_pair(earlier_pair, later_pair):
    return (earlier_pair[0] + later_pair[0], earlier_pair[1] + later_pair[1])


def per_device(queries, keys, values, out_weight):
    local_rows = queries.shape[1]
    feature_width = queries.shape[2]
    head_count = feature_width // CHANNEL_WIDTH
    local_blocks = local_rows // SEGMENT_LENGTH
    shard_count = lax.axis_size("seq")
    shard_index = lax.axis_index("seq")
    total_blocks = local_blocks * shard_count
    first_block = shard_index * local_blocks
    softmax_multiplier = 1.0 / math.sqrt(CHANNEL_WIDTH)
    faraway_offset_bias = math.log(SEGMENT_LENGTH)
    own_queries = queries[0]
    own_keys = keys[0]
    own_values = values[0]
    span_address_means = jnp.mean(
        own_keys.reshape(local_blocks, SEGMENT_LENGTH, feature_width), axis=1, dtype=jnp.float32
    ).astype(jnp.bfloat16)
    value_means = jnp.mean(
        own_values.reshape(local_blocks, SEGMENT_LENGTH, feature_width), axis=1, dtype=jnp.float32
    ).astype(jnp.bfloat16)
    empty_buffer = jnp.zeros((total_blocks, feature_width), jnp.bfloat16)
    slot_keys = lax.dynamic_update_slice_in_dim(empty_buffer, span_address_means, first_block, 0)
    slot_values = lax.dynamic_update_slice_in_dim(empty_buffer, value_means, first_block, 0)
    far_keys, far_values = prefix(
        (slot_keys, slot_values), "seq", add_pair, (empty_buffer, empty_buffer)
    )
    prev_keys, prev_values = shifted(
        (own_keys[local_rows - SEGMENT_LENGTH :], own_values[local_rows - SEGMENT_LENGTH :]),
        "seq",
        1,
    )
    near_keys = jnp.concatenate([prev_keys, own_keys], axis=0)
    near_values = jnp.concatenate([prev_values, own_values], axis=0)
    far_k = far_keys.reshape(total_blocks, head_count, CHANNEL_WIDTH)
    far_v = far_values.reshape(total_blocks, head_count, CHANNEL_WIDTH)
    far_index = jnp.arange(total_blocks, dtype=jnp.int32)
    group_rows = SEGMENT_LENGTH * math.gcd(local_blocks, max(1, 512 // SEGMENT_LENGTH))
    request_vectors = own_queries.reshape(group_rows, head_count, CHANNEL_WIDTH)
    address_vectors = near_keys.reshape(group_rows + SEGMENT_LENGTH, head_count, CHANNEL_WIDTH)
    value_rows = near_values.reshape(group_rows + SEGMENT_LENGTH, head_count, CHANNEL_WIDTH)
    query_local = 0 + jnp.arange(group_rows, dtype=jnp.int32)
    key_local = 0 - SEGMENT_LENGTH + jnp.arange(group_rows + SEGMENT_LENGTH, dtype=jnp.int32)
    query_blk = query_local // SEGMENT_LENGTH
    key_blk = key_local // SEGMENT_LENGTH
    within_block = (key_blk[None, :] == query_blk[:, None]) & (
        key_local[None, :] <= query_local[:, None]
    )
    preceding_segment = (key_blk[None, :] == query_blk[:, None] - 1) & (
        (key_blk[None, :] >= 0) | (shard_index > 0)
    )
    adjacent_similarity = (
        jnp.einsum(
            "qhd,khd->hqk", request_vectors, address_vectors, preferred_element_type=jnp.float32
        )
        * softmax_multiplier
    )
    adjacent_similarity = jnp.where(
        (within_block | preceding_segment)[None], adjacent_similarity, -jnp.inf
    )
    query_global = first_block + query_blk
    faraway_similarity = (
        jnp.einsum("qhd,jhd->hqj", request_vectors, far_k, preferred_element_type=jnp.float32)
        * softmax_multiplier
        + faraway_offset_bias
    )
    faraway_similarity = jnp.where(
        (far_index[None, :] < query_global[:, None] - 1)[None], faraway_similarity, -jnp.inf
    )
    row_max = jnp.maximum(
        jnp.max(adjacent_similarity, axis=-1), jnp.max(faraway_similarity, axis=-1)
    )[..., None]
    near_w = jnp.exp(adjacent_similarity - row_max)
    far_w = jnp.exp(faraway_similarity - row_max)
    row_total = jnp.sum(near_w, axis=-1, keepdims=True) + jnp.sum(far_w, axis=-1, keepdims=True)
    near_p = (near_w / row_total).astype(jnp.bfloat16)
    far_p = (far_w / row_total).astype(jnp.bfloat16)
    attended = jnp.einsum("hqk,khd->qhd", near_p, value_rows, preferred_element_type=jnp.float32)
    attended = attended + jnp.einsum(
        "hqj,jhd->qhd", far_p, far_v, preferred_element_type=jnp.float32
    )
    pieces = attended.astype(jnp.bfloat16).reshape(group_rows, feature_width)
    projected = jnp.dot(
        pieces,
        lax.all_gather(out_weight, "dp", axis=1, tiled=True),
        preferred_element_type=jnp.float32,
    ).astype(jnp.bfloat16)
    return projected[None]


def solution(mesh):
    return jax.shard_map(
        per_device,
        mesh=mesh,
        in_specs=(P("dp", "seq", None), P("dp", "seq", None), P("dp", "seq", None), P(None, "dp")),
        out_specs=P("dp", "seq", None),
        check_vma=False,
    )
```

profile of v0, /device:TPU:1, one launch (start us, length us, event | category | flops | bytes accessed | tf_op | source)
XLA Modules:
  0.0 340.8 jit_solution(379502660158891560)
XLA Ops:
  6.5 2.1 convert_reduce_fusion.1
  11.4 3.9 %copy.25 = bf16[1,512,2048]{1,2,0:T(8,128)(2,1)} copy(bf16[1,512,2048]{2,1,0:T(8,128)(2,1)} %param.7) | data formatting | bytes 4194304 | tf_op args[1]
  15.4 2.3 slice_bitcast_fusion
  17.7 4.6 %collective-permute-start.1 = (bf16[256,2048]{0,1:T(8,128)(2,1)}, bf16[256,2048]{0,1:T(8,128)(2,1)}, u32[]{:S(2)}, u32[]{:S(2)}) collective-permute-start(bf16[256,2048]{0,1:T(8,128)(2,1)} %slice_bitcast_fusion), channel_id=1, source_target_pairs={{0,8},{8,16},{16,24},{24,32},{32,40},{40,48},{48,56},{56,64},{64,7... | collective-permute-start | bytes 3145736 | tf_op jit(solution)/shard_map/ppermute | solution.py:28
  23.3 1.9 collective-permute-start
  25.2 2.5 copy.24
  27.7 3.7 %copy.37 = bf16[64,8,16,128]{3,2,1,0:T(8,128)(2,1)} copy(bf16[64,8,16,128]{3,1,2,0:T(8,128)(2,1)} %bitcast.68) | data formatting | bytes 4194304
  31.4 2.4 copy.28
  34.7 3.3 collective-permute-done.1
  38.1 2.3 copy.27
  40.3 9.4 %collective-permute-done = bf16[256,2048]{1,0:T(8,128)(2,1)} collective-permute-done((bf16[256,2048]{1,0:T(8,128)(2,1)}, bf16[256,2048]{1,0:T(8,128)(2,1)}, u32[]{:S(2)}, u32[]{:S(2)}) %collective-permute-start) | collective-permute-done | bytes 1048608 | tf_op jit(solution)/shard_map/ppermute | solution.py:28
  49.7 2.3 copy.23
  52.0 12.3 %fusion.1 = (f32[16,512]{1,0:T(8,128)S(1)}, f32[16,768,512]{2,1,0:T(8,128)}) fusion(pred[512,768]{0,1:T(8,128)(4,1)S(1)} %fusion.20, bf16[512,16,128]{2,1,0:T(8,128)(2,1)S(1)} %bitcast.70, bf16[512,16,128]{2,0,1:T(8,128)(2,1)} %copy.28, bf16[256,16,128]{2,0,1:T(8,128)(2,1)} %copy.27), kind=kOutput, calls=%fused_computation.6 | convolution fusion | flops 1635770368 | bytes 30834688 | tf_op jit(solution)/shard_map/qhd,khd->hqk/dot_general | solution.py:86
  64.3 21.8 %all-gather.4.cloned.1.call-done = bf16[32,64,2048]{2,1,0:T(8,128)(2,1)} async-done(((bf16[1,64,2048]{2,1,0:T(8,128)(2,1)}), bf16[32,64,2048]{2,1,0:T(8,128)(2,1)}) %all-gather.4.cloned.1.call-update) | async-done | bytes 8388624 | tf_op jit(solution)/shard_map/all_gather | solution.py:13
  86.1 60.0 %all-gather.6.cloned.1.call-done = bf16[32,64,2048]{2,1,0:T(8,128)(2,1)} async-done(((bf16[1,64,2048]{2,1,0:T(8,128)(2,1)}), bf16[32,64,2048]{2,1,0:T(8,128)(2,1)}) %all-gather.6.cloned.1.call-update) | async-done | bytes 8388624 | tf_op jit(solution)/shard_map/all_gather | solution.py:13
  146.2 39.2 %while.16 = (s32[]{:T(128)}, bf16[64,2048]{1,0:T(8,128)(2,1)S(1)}, bf16[64,2048]{1,0:T(8,128)(2,1)S(1)}, s32[]{:T(128)}, bf16[32,64,2048]{2,1,0:T(8,128)(2,1)}, ...) while((s32[]{:T(128)}, bf16[64,2048]{1,0:T(8,128)(2,1)S(1)}, ...), condition=%wide.region_4.5_spmd.clone, body=%wide.region_3.4_spmd.clone.sunk | while | flops 786436 | bytes 1572973 | solution.py:22
  147.4 1.2 add_select_fusion.5
  148.7 1.2 add_select_fusion.5
  149.9 1.2 add_select_fusion.5
  151.2 1.2 add_select_fusion.5
  152.5 1.2 add_select_fusion.5
  155.0 1.2 add_select_fusion.5
  156.2 1.2 add_select_fusion.5
  158.8 1.3 add_select_fusion.5
  160.1 1.3 add_select_fusion.5
  161.4 1.2 add_select_fusion.5
  163.9 1.2 add_select_fusion.5
  165.2 1.2 add_select_fusion.5
  166.4 1.2 add_select_fusion.5
  167.7 1.2 add_select_fusion.5
  168.9 1.2 add_select_fusion.5
  170.2 1.2 add_select_fusion.5
  171.5 1.2 add_select_fusion.5
  172.7 1.2 add_select_fusion.5
  174.0 1.2 add_select_fusion.5
  175.3 1.2 add_select_fusion.5
  176.5 1.2 add_select_fusion.5
  177.8 1.2 add_select_fusion.5
  179.1 1.2 add_select_fusion.5
  180.3 1.2 add_select_fusion.5
  181.6 1.2 add_select_fusion.5
  182.9 1.2 add_select_fusion.5
  185.4 1.5 fusion.42
  187.3 11.3 %fusion = f32[16,512]{1,0:T(8,128)S(1)} fusion(f32[16,768,512]{2,1,0:T(8,128)} %get-tuple-element.153, f32[16,512]{1,0:T(8,128)S(1)} %max.7, pred[512,768]{0,1:T(8,128)(4,1)S(1)} %fusion.20), kind=kLoop, calls=%fused_computation.5 | loop fusion | flops 25157632 | bytes 25624576 | tf_op jit(solution)/shard_map/reduce_sum | solution.py:108
  198.5 2.8 fusion.21
  201.3 14.6 %add_convert_fusion = bf16[16,128,512]{2,1,0:T(8,128)(2,1)} fusion(f32[16,128,512]{2,1,0:T(8,128)} %fusion.21, f32[16,768,512]{2,1,0:T(8,128)} %get-tuple-element.153, f32[16,512]{1,0:T(8,128)S(1)} %add.130, f32[16,512]{1,0:T(8,128)S(1)} %max.7, pred[512,768]{0,1:T(8,128)(4,1)S(1)} %fusion.20, bf16[512,16,128]{0,2,1:T(8,128)(2,1)S(1)} %bitcast.69, ...), kind=kOutput, calls=%fused_computation.12 | convolution fusion | flops 1650458624 | bytes 35061760 | tf_op jit(solution)/shard_map/hqk,khd->qhd/dot_general | solution.py:111
  215.9 103.9 %all-gather.8.cloned.1.call-done = bf16[2048,4096]{1,0:T(8,128)(2,1)} async-done(((bf16[2048,512]{1,0:T(8,128)(2,1)}), bf16[2048,4096]{1,0:T(8,128)(2,1)}) %all-gather.8.cloned.1.call-update) | async-done | bytes 16777232 | tf_op jit(solution)/shard_map/all_gather | solution.py:118
  319.8 14.5 %fusion.3 = bf16[1,512,4096]{2,1,0:T(8,128)(2,1)} fusion(bf16[512,2048]{0,1:T(8,128)(2,1)} %bitcast.73, bf16[2048,4096]{1,0:T(8,128)(2,1)} %all-gather.8.cloned.1.call-done), kind=kOutput, calls=%fused_computation.9 | convolution fusion | flops 8592031744 | bytes 23068672 | tf_op jit(solution)/shard_map/dot_general | solution.py:116
  (40 shorter events, 11.2 us)
Async XLA Ops:
  6.5 3.0 copy-start
  6.5 79.6 %all-gather.4.cloned.1.call-start = ((), (), s32[]{:S(2)}) async-start(), calls=%async_computation | async-start | bytes 8650752 | tf_op jit(solution)/shard_map/all_gather | solution.py:13
  8.7 0.7 copy-start.5
  9.5 136.7 %all-gather.6.cloned.1.call-start = ((), (), s32[]{:S(2)}) async-start(), calls=%async_computation.1 | async-start | bytes 8650752 | tf_op jit(solution)/shard_map/all_gather | solution.py:13
  10.0 0.7 copy-start.4
  10.7 309.1 %all-gather.8.cloned.1.call-start = ((), (), s32[]{:S(2)}) async-start(), calls=%async_computation.2 | async-start | bytes 18874368 | tf_op jit(solution)/shard_map/all_gather | solution.py:118
  17.7 20.4 %collective-permute-start.1 = (bf16[256,2048]{0,1:T(8,128)(2,1)}, bf16[256,2048]{0,1:T(8,128)(2,1)}, u32[]{:S(2)}, u32[]{:S(2)}) collective-permute-start(bf16[256,2048]{0,1:T(8,128)(2,1)} %slice_bitcast_fusion), channel_id=1, source_target_pairs={{0,8},{8,16},{16,24},{24,32},{32,40},{40,48},{48,56},{56,64},{64,7... | collective-permute-start | bytes 3145736 | tf_op jit(solution)/shard_map/ppermute | solution.py:28
  23.3 26.4 %collective-permute-start = (bf16[256,2048]{1,0:T(8,128)(2,1)}, bf16[256,2048]{1,0:T(8,128)(2,1)}, u32[]{:S(2)}, u32[]{:S(2)}) collective-permute-start(bf16[256,2048]{1,0:T(8,128)(2,1)} %slice_bitcast_fusion.1), channel_id=1, source_target_pairs={{0,8},{8,16},{16,24},{24,32},{32,40},{40,48},{48,56},{56,64},{64,7... | collective-permute-start | bytes 3145736 | tf_op jit(solution)/shard_map/ppermute | solution.py:28
  27.7 3.7 %copy-start.1 = (bf16[1,512,2048]{1,2,0:T(8,128)(2,1)S(1)}, bf16[1,512,2048]{1,2,0:T(8,128)(2,1)}, u32[]{:S(2)}) copy-start(bf16[1,512,2048]{1,2,0:T(8,128)(2,1)} %copy.25) | copy-start | bytes 6291460
  33.8 18.2 %copy-start.3 = (bf16[64,8,16,128]{3,2,1,0:T(8,128)(2,1)S(1)}, bf16[64,8,16,128]{3,2,1,0:T(8,128)(2,1)}, u32[]{:S(2)}) copy-start(bf16[64,8,16,128]{3,2,1,0:T(8,128)(2,1)} %copy.37) | copy-start | bytes 6291460
  198.5 2.8 copy-start.2
Sparse Core Ops, SparseCore 0:
  9.9 76.2 all-gather.3
  88.7 57.4 all-gather.5
  148.0 171.7 all-gather.7
where the time goes:
time: 342 us; the launch traced here: 341 us
  waiting for transfers between devices  199 us (58%)
  other arithmetic  53.6 us (16%)
  matrix products  45.6 us (13%)
  local copies, waits for them, and re-layouts  21.8 us (6%)
  between operations  13.3 us (4%)
  starting transfers between devices  6.57 us (2%)
    all_gather x1, waiting for transfers between devices, per_device(): lax.all_gather(out_weight, 'dp', axis=1, tiled=True)  104 us
    all_gather x2, waiting for transfers between devices, prefix(): pieces = jax.tree.map(lambda part: lax.all_gather(part, axis), value)  81.8 us
    select_n x31, other arithmetic, turn(): jnp.where(position < mine, new, old)  38.5 us
    dot_general x1, matrix products, per_device(): jnp.einsum('hqk,khd->qhd', near_p, value_rows, preferred_element_type=jnp...  14.6 us
    dot_general x1, matrix products, per_device(): jnp.dot(pieces, lax.all_gather(out_weight, 'dp', axis=1, tiled=True), pre...  14.5 us
    ppermute x2, waiting for transfers between devices, shifted(): return lax.ppermute(block, axis, route)  12.7 us
    dot_general x1, matrix products, per_device(): jnp.einsum('qhd,khd->hqk', request_vectors, address_vectors, preferred_el...  12.3 us
    unnamed x15, local copies, waits for them, and re-layouts  11.5 us
  transfers between devices with their start and end apart: 5, of which 5 were waited for; matrix products, arithmetic and copies ran while one was open for 30% of the time, Pallas kernels for 0%

commit v1 on v0

--- a/solution.py
+++ b/solution.py
@@ -6,6 +6,11 @@
 
 CHANNEL_WIDTH = 128
 SEGMENT_LENGTH = 256
+
+
+def tiled_gather(shard, axis, dim):
+    copies = jnp.concatenate([shard] * lax.axis_size(axis), axis=dim)
+    return lax.all_to_all(copies, axis, dim, dim, tiled=True)
 
 
 def prefix(value, axis, join, neutral):
@@ -114,9 +119,7 @@
     )
     pieces = attended.astype(jnp.bfloat16).reshape(group_rows, feature_width)
     projected = jnp.dot(
-        pieces,
-        lax.all_gather(out_weight, "dp", axis=1, tiled=True),
-        preferred_element_type=jnp.float32,
+        pieces, tiled_gather(out_weight, "dp", 1), preferred_element_type=jnp.float32
     ).astype(jnp.bfloat16)
     return projected[None]
 

time: 342 us -> 464 us (1.36)
  waiting for transfers between devices: 199 us -> 258 us
  local copies, waits for them, and re-layouts: 21.8 us -> 75.1 us
  starting transfers between devices: 6.57 us -> 15.2 us
    all_to_all x0 -> x1, waiting for transfers between devices: none -> 217 us  [tiled_gather(): return lax.all_to_all(copies, axis, dim, dim, tiled=True)]
    all_gather x1 -> x0, waiting for transfers between devices: 104 us -> none  [per_device(): lax.all_gather(out_weight, 'dp', axis=1, tiled=True)]
    all_gather x2, waiting for transfers between devices: 81.8 us -> 28.5 us  [prefix(): pieces = jax.tree.map(lambda part: lax.all_gather(part, axis), value)]
    all_to_all x0 -> x2, local copies, waits for them, and re-layouts: none -> 43.2 us  [tiled_gather(): return lax.all_to_all(copies, axis, dim, dim, tiled=True)]
    unnamed x15 -> x27, local copies, waits for them, and re-layouts: 11.5 us -> 21.4 us
    all_to_all x0 -> x1, starting transfers between devices: none -> 8.97 us  [tiled_gather(): return lax.all_to_all(copies, axis, dim, dim, tiled=True)]
  transfers between devices with their start and end apart: 5 -> 5, of which waited for: 5 -> 4; matrix products, arithmetic and copies ran while one was open for 30% -> 28% of each run, Pallas kernels for 0% -> 0%
where the time goes in v1:
time: 464 us; the launch traced here: 462 us
  waiting for transfers between devices  258 us (56%)
  local copies, waits for them, and re-layouts  75.1 us (16%)
  other arithmetic  54.7 us (12%)
  matrix products  44.5 us (10%)
  starting transfers between devices  15.2 us (3%)
  between operations  13.7 us (3%)
    all_to_all x1, waiting for transfers between devices, tiled_gather(): return lax.all_to_all(copies, axis, dim, dim, tiled=True)  217 us
    all_to_all x2, local copies, waits for them, and re-layouts, tiled_gather(): return lax.all_to_all(copies, axis, dim, dim, tiled=True)  43.2 us
    select_n x31, other arithmetic, turn(): jnp.where(position < mine, new, old)  38.3 us
    all_gather x2, waiting for transfers between devices, prefix(): pieces = jax.tree.map(lambda part: lax.all_gather(part, axis), value)  28.5 us
    unnamed x27, local copies, waits for them, and re-layouts  21.4 us
    dot_general x1, matrix products, per_device(): jnp.einsum('hqk,khd->qhd', near_p, value_rows, preferred_element_type=jnp...  14.3 us
    dot_general x1, matrix products, per_device(): jnp.dot(pieces, tiled_gather(out_weight, 'dp', 1), preferred_element_type...  13.8 us
    ppermute x2, waiting for transfers between devices, shifted(): return lax.ppermute(block, axis, route)  12.6 us
  transfers between devices with their start and end apart: 5, of which 4 were waited for; matrix products, arithmetic and copies ran while one was open for 28% of the time, Pallas kernels for 0%

profile of v1, /device:TPU:1, one launch (start us, length us, event | category | flops | bytes accessed | tf_op | source)
XLA Modules:
  0.0 462.1 jit_solution(2368963682081632369)
XLA Ops:
  6.5 2.0 convert_reduce_fusion.1
  9.3 2.0 convert_reduce_fusion
  12.1 2.9 copy.45
  16.2 5.7 %copy-done = bf16[2048,4096]{0,1:T(8,128)(2,1)} copy-done((bf16[2048,4096]{0,1:T(8,128)(2,1)}, bf16[2048,4096]{0,1:T(8,128)(2,1)S(1)}, u32[]{:S(2)}) %copy-start) | copy-done | bytes 16777240
  22.0 21.7 %copy.53 = bf16[2048,8,512]{2,0,1:T(8,128)(2,1)} copy(bf16[2048,8,512]{0,2,1:T(8,128)(2,1)} %bitcast.67) | data formatting | bytes 33554432 | tf_op jit(solution)/shard_map/all_to_all | solution.py:13
  43.6 9.0 %all-to-all-start = ((bf16[2048,8,512]{2,0,1:T(8,128)(2,1)}), bf16[2048,8,512]{2,0,1:T(8,128)(2,1)}, u32[]{:S(2)}, u32[]{:S(2)}) async-start(bf16[2048,8,512]{2,0,1:T(8,128)(2,1)} %copy.53), calls=%async_computation | async-start | bytes 33554432 | tf_op jit(solution)/shard_map/all_to_all | solution.py:13
  52.6 4.1 copy.36
  56.7 2.3 slice_bitcast_fusion
  59.0 4.1 collective-permute-start.1
  64.2 2.1 collective-permute-start
  66.3 2.6 copy.35
  68.8 3.7 copy.58
  72.5 2.4 copy.39
  75.8 2.2 collective-permute-done.1
  78.1 2.2 copy.38
  80.3 10.4 %collective-permute-done = bf16[256,2048]{1,0:T(8,128)(2,1)} collective-permute-done((bf16[256,2048]{1,0:T(8,128)(2,1)}, bf16[256,2048]{1,0:T(8,128)(2,1)}, u32[]{:S(2)}, u32[]{:S(2)}) %collective-permute-start) | collective-permute-done | bytes 1048608 | tf_op jit(solution)/shard_map/ppermute | solution.py:33
  90.7 2.3 copy.34
  93.0 12.2 %fusion.1 = (f32[16,512]{1,0:T(8,128)S(1)}, f32[16,768,512]{2,1,0:T(8,128)}) fusion(pred[512,768]{0,1:T(8,128)(4,1)S(1)} %fusion.20, bf16[512,16,128]{2,1,0:T(8,128)(2,1)S(1)} %bitcast.74, bf16[512,16,128]{2,0,1:T(8,128)(2,1)} %copy.39, bf16[256,16,128]{2,0,1:T(8,128)(2,1)} %copy.38), kind=kOutput, calls=%fused_computation.6 | convolution fusion | flops 1635770368 | bytes 30834688 | tf_op jit(solution)/shard_map/qhd,khd->hqk/dot_general | solution.py:91
  105.2 28.5 %all-gather.5.cloned.1.call-done = bf16[32,64,2048]{2,1,0:T(8,128)(2,1)} async-done(((bf16[1,64,2048]{2,1,0:T(8,128)(2,1)}), bf16[32,64,2048]{2,1,0:T(8,128)(2,1)}) %all-gather.5.cloned.1.call-update) | async-done | bytes 8388624 | tf_op jit(solution)/shard_map/all_gather | solution.py:18
  133.7 39.1 %while.16 = (s32[]{:T(128)}, bf16[64,2048]{1,0:T(8,128)(2,1)S(1)}, bf16[64,2048]{1,0:T(8,128)(2,1)S(1)}, s32[]{:T(128)}, bf16[32,64,2048]{2,1,0:T(8,128)(2,1)}, ...) while((s32[]{:T(128)}, bf16[64,2048]{1,0:T(8,128)(2,1)S(1)}, ...), condition=%wide.region_4.5_spmd.clone, body=%wide.region_3.4_spmd.clone.sunk | while | flops 786436 | bytes 1572973 | solution.py:27
  135.0 1.2 add_select_fusion.5
  136.2 1.2 add_select_fusion.5
  137.5 1.2 add_select_fusion.5
  138.7 1.2 add_select_fusion.5
  140.0 1.2 add_select_fusion.5
  142.5 1.2 add_select_fusion.5
  143.8 1.2 add_select_fusion.5
  146.3 1.2 add_select_fusion.5
  147.6 1.2 add_select_fusion.5
  150.1 1.2 add_select_fusion.5
  151.3 1.2 add_select_fusion.5
  153.9 1.2 add_select_fusion.5
  155.1 1.2 add_select_fusion.5
  156.4 1.2 add_select_fusion.5
  157.6 1.2 add_select_fusion.5
  158.9 1.2 add_select_fusion.5
  160.2 1.2 add_select_fusion.5
  161.4 1.2 add_select_fusion.5
  162.7 1.2 add_select_fusion.5
  163.9 1.2 add_select_fusion.5
  166.5 1.2 add_select_fusion.5
  172.8 1.5 fusion.42
  174.6 11.1 %fusion = f32[16,512]{1,0:T(8,128)S(1)} fusion(f32[16,768,512]{2,1,0:T(8,128)} %get-tuple-element.153, f32[16,512]{1,0:T(8,128)S(1)} %max.7, pred[512,768]{0,1:T(8,128)(4,1)S(1)} %fusion.20), kind=kLoop, calls=%fused_computation.5 | loop fusion | flops 25157632 | bytes 25624576 | tf_op jit(solution)/shard_map/reduce_sum | solution.py:113
  185.8 2.8 fusion.21
  188.6 14.3 %add_convert_fusion = bf16[16,128,512]{2,1,0:T(8,128)(2,1)} fusion(f32[16,128,512]{2,1,0:T(8,128)} %fusion.21, f32[16,768,512]{2,1,0:T(8,128)} %get-tuple-element.153, f32[16,512]{1,0:T(8,128)S(1)} %add.130, f32[16,512]{1,0:T(8,128)S(1)} %max.7, pred[512,768]{0,1:T(8,128)(4,1)S(1)} %fusion.20, bf16[512,16,128]{0,2,1:T(8,128)(2,1)S(1)} %bitcast.73, ...), kind=kOutput, calls=%fused_computation.12 | convolution fusion | flops 1650458624 | bytes 35061760 | tf_op jit(solution)/shard_map/hqk,khd->qhd/dot_general | solution.py:116
  202.9 217.0 %all-to-all-done = bf16[2048,8,512]{2,0,1:T(8,128)(2,1)} async-done(((bf16[2048,8,512]{2,0,1:T(8,128)(2,1)}), bf16[2048,8,512]{2,0,1:T(8,128)(2,1)}, u32[]{:S(2)}, u32[]{:S(2)}) %all-to-all-start) | async-done | bytes 16777248 | tf_op jit(solution)/shard_map/all_to_all | solution.py:13
  419.8 21.6 %copy.54 = bf16[2048,8,512]{0,2,1:T(8,128)(2,1)} copy(bf16[2048,8,512]{2,0,1:T(8,128)(2,1)} %all-to-all-done) | data formatting | bytes 33554432 | tf_op jit(solution)/shard_map/all_to_all | solution.py:13
  441.4 13.8 %fusion.3 = bf16[1,512,4096]{2,1,0:T(8,128)(2,1)} fusion(bf16[512,2048]{0,1:T(8,128)(2,1)S(1)} %bitcast.77, bf16[2048,4096]{0,1:T(8,128)(2,1)} %bitcast.68), kind=kOutput, calls=%fused_computation.9 | convolution fusion | flops 8592031744 | bytes 23068672 | tf_op jit(solution)/shard_map/dot_general | solution.py:121
  (54 shorter events, 17.4 us)
Async XLA Ops:
  6.5 98.6 %all-gather.3.cloned.1.call-start = ((), (), s32[]{:S(2)}) async-start(), calls=%async_computation.1 | async-start | bytes 8650752 | tf_op jit(solution)/shard_map/all_gather | solution.py:18
  8.6 0.7 copy-start.6
  9.3 124.4 %all-gather.5.cloned.1.call-start = ((), (), s32[]{:S(2)}) async-start(), calls=%async_computation.2 | async-start | bytes 8650752 | tf_op jit(solution)/shard_map/all_gather | solution.py:18
  11.4 0.7 copy-start.5
  16.2 5.7 %copy-start = (bf16[2048,4096]{0,1:T(8,128)(2,1)}, bf16[2048,4096]{0,1:T(8,128)(2,1)S(1)}, u32[]{:S(2)}) copy-start(bf16[2048,4096]{0,1:T(8,128)(2,1)S(1)} %constant_dynamic-update-slice_fusion) | copy-start | bytes 50331652
  43.6 376.2 %all-to-all-start = ((bf16[2048,8,512]{2,0,1:T(8,128)(2,1)}), bf16[2048,8,512]{2,0,1:T(8,128)(2,1)}, u32[]{:S(2)}, u32[]{:S(2)}) async-start(bf16[2048,8,512]{2,0,1:T(8,128)(2,1)} %copy.53), calls=%async_computation | async-start | bytes 33554432 | tf_op jit(solution)/shard_map/all_to_all | solution.py:13
  52.6 10.5 %copy-start.1 = (bf16[1,512,2048]{2,1,0:T(8,128)(2,1)S(1)}, bf16[1,512,2048]{2,1,0:T(8,128)(2,1)}, u32[]{:S(2)}) copy-start(bf16[1,512,2048]{2,1,0:T(8,128)(2,1)} %param.8) | copy-start | bytes 6291460
  59.0 19.0 %collective-permute-start.1 = (bf16[256,2048]{0,1:T(8,128)(2,1)}, bf16[256,2048]{0,1:T(8,128)(2,1)}, u32[]{:S(2)}, u32[]{:S(2)}) collective-permute-start(bf16[256,2048]{0,1:T(8,128)(2,1)} %slice_bitcast_fusion), channel_id=1, source_target_pairs={{0,8},{8,16},{16,24},{24,32},{32,40},{40,48},{48,56},{56,64},{64,7... | collective-permute-start | bytes 3145736 | tf_op jit(solution)/shard_map/ppermute | solution.py:33
  64.2 26.5 %collective-permute-start = (bf16[256,2048]{1,0:T(8,128)(2,1)}, bf16[256,2048]{1,0:T(8,128)(2,1)}, u32[]{:S(2)}, u32[]{:S(2)}) collective-permute-start(bf16[256,2048]{1,0:T(8,128)(2,1)} %slice_bitcast_fusion.1), channel_id=1, source_target_pairs={{0,8},{8,16},{16,24},{24,32},{32,40},{40,48},{48,56},{56,64},{64,7... | collective-permute-start | bytes 3145736 | tf_op jit(solution)/shard_map/ppermute | solution.py:33
  68.8 3.7 copy-start.2
  74.9 18.1 %copy-start.4 = (bf16[64,8,16,128]{3,2,1,0:T(8,128)(2,1)S(1)}, bf16[64,8,16,128]{3,2,1,0:T(8,128)(2,1)}, u32[]{:S(2)}) copy-start(bf16[64,8,16,128]{3,2,1,0:T(8,128)(2,1)} %copy.58) | copy-start | bytes 6291460
  185.8 2.8 copy-start.3
  202.9 238.5 %copy-start.7 = (bf16[16,128,512]{2,1,0:T(8,128)(2,1)S(1)}, bf16[16,128,512]{2,1,0:T(8,128)(2,1)}, u32[]{:S(2)}) copy-start(bf16[16,128,512]{2,1,0:T(8,128)(2,1)} %add_convert_fusion) | copy-start | bytes 6291460
Sparse Core Ops, SparseCore 0:
  9.9 61.9 all-gather.2
  74.5 59.1 all-gather.4
